TPU v7x, 128 devices: a whole 4x4x4 slice. The times are simulated.
128 devices in a mesh: gx: 16 (over z_hi, x, core), gy: 4 (over y), gz: 2 (over z_lo).
Axes of the slice: x: 4, y: 4, z: 4 (z_hi: 2, z_lo: 2; z = z_hi * 2 + z_lo), core: 2. Of those that a mesh axis runs over, the one named last changes fastest.
Arguments:
- cells: bfloat16 [4, 64, 256, 256], P(None, 'gx', 'gy', 'gz'), may hold values from -6 to 6
- weight: bfloat16 [32, 4, 3, 3, 3], replicated, may hold values from -0.625 to 0.625
- bias: float32 [32], replicated, may hold values from -3 to 3
- cotangent: bfloat16 [32, 32, 128, 128], P(None, 'gx', 'gy', 'gz'), may hold values from -6 to 6
Outputs:
- pooled: bfloat16 [32, 32, 128, 128], P(None, 'gx', 'gy', 'gz')
- weight_grad: float32 [32, 4, 3, 3, 3], replicated
- bias_grad: float32 [32], replicated
- input_grad: float32 [4, 64, 256, 256], P(None, 'gx', 'gy', 'gz')
All inputs are finite; a program needn't handle non-finite values.
Results may differ from a plain program's by a relative error of at most 0.0029.
Values may be sent and summed in bfloat16 or wider, within the bound.
A program may use at most 128 MiB of HBM per device.

v0:
```python
import jax
import jax.numpy as jnp
from jax import lax
from jax.sharding import PartitionSpec as P

leak_slope = 0.3
soft_scale = 10.0


def extended(cells, sides, width):
    for axis, dim in sides:
        count = lax.axis_size(axis)
        head = lax.slice_in_dim(cells, 0, width, axis=dim)
        tail = lax.slice_in_dim(cells, cells.shape[dim] - width, cells.shape[dim], axis=dim)
        cells = jnp.concatenate(
            [
                lax.ppermute(tail, axis, [(i, (i + 1) % count) for i in range(count)]),
                cells,
                lax.ppermute(head, axis, [((i + 1) % count, i) for i in range(count)]),
            ],
            axis=dim,
        )
    return cells


def activate(preact):
    return leak_slope * preact + (1.0 - leak_slope) / soft_scale * jax.nn.softplus(
        soft_scale * preact
    )


def slope_of(preact):
    return leak_slope + (1.0 - leak_slope) * jax.nn.sigmoid(soft_scale * preact)


def on_device(cells, weight, bias, cotangent):
    chan_in, cells_x, cells_y, cells_z = cells.shape
    chan_out = weight.shape[0]
    stencil = [
        (shift_a, shift_b, shift_e)
        for shift_a in range(3)
        for shift_b in range(3)
        for shift_e in range(3)
    ]
    widened = extended(cells, (("gx", 1), ("gy", 2), ("gz", 3)), 1)
    patches = jnp.stack(
        [
            widened[:, sa : sa + cells_x, sb : sb + cells_y, se : se + cells_z]
            for sa, sb, se in stencil
        ],
        axis=1,
    )
    patches = patches.reshape(chan_in * 27, cells_x, cells_y, cells_z)
    weight_mat = weight.reshape(chan_out, chan_in * 27)
    preact = (
        jnp.einsum("ok,kxyz->oxyz", weight_mat, patches, preferred_element_type=jnp.float32)
        + bias[:, None, None, None]
    )
    activated = activate(preact)
    pooled = (
        activated.reshape(chan_out, cells_x // 2, 2, cells_y // 2, 2, cells_z // 2, 2)
        .mean(axis=(2, 4, 6))
        .astype(jnp.bfloat16)
    )
    spread = jnp.broadcast_to(
        cotangent.astype(jnp.float32)[:, :, None, :, None, :, None],
        (chan_out, cells_x // 2, 2, cells_y // 2, 2, cells_z // 2, 2),
    )
    spread = spread.reshape(chan_out, cells_x, cells_y, cells_z)
    delta = (slope_of(preact) * spread * 0.125).astype(jnp.bfloat16)
    weight_local = jnp.einsum("oxyz,kxyz->ok", delta, patches, preferred_element_type=jnp.float32)
    bias_local = jnp.sum(delta, axis=(1, 2, 3), dtype=jnp.float32)
    weight_total, bias_grad = lax.psum((weight_local, bias_local), ("gx", "gy", "gz"))
    weight_grad = weight_total.reshape(chan_out, chan_in, 3, 3, 3)
    delta_wide = extended(delta, (("gx", 1), ("gy", 2), ("gz", 3)), 1)
    input_grad = jnp.zeros((chan_in, cells_x, cells_y, cells_z), jnp.float32)
    for sa, sb, se in stencil:
        window = delta_wide[:, sa : sa + cells_x, sb : sb + cells_y, se : se + cells_z]
        input_grad = input_grad + jnp.einsum(
            "oc,oxyz->cxyz",
            weight[:, :, 2 - sa, 2 - sb, 2 - se],
            window,
            preferred_element_type=jnp.float32,
        )
    return (pooled, weight_grad, bias_grad, input_grad)


def solution(mesh):
    in_specs = (P(None, "gx", "gy", "gz"), P(), P(), P(None, "gx", "gy", "gz"))
    out_specs = (P(None, "gx", "gy", "gz"), P(), P(), P(None, "gx", "gy", "gz"))
    return jax.shard_map(
        on_device, mesh=mesh, in_specs=in_specs, out_specs=out_specs, check_vma=False
    )
```

profile of v0, /device:TPU:0, one launch (start us, length us, event | category | flops | bytes accessed | tf_op | source)
XLA Modules:
  0.0 232.9 jit_solution(10944951480757157942)
XLA Ops:
  1.6 5.7 %collective-permute-start.1 = (bf16[4,1,64,128]{3,2,1,0:T(8,128)(2,1)S(1)}, bf16[4,1,64,128]{3,2,1,0:T(8,128)(2,1)S(1)}, u32[]{:S(2)}, u32[]{:S(2)}) collective-permute-start(bf16[4,1,64,128]{3,2,1,0:T(8,128)(2,1)S(1)} %get-tuple-element.35), channel_id=1, source_target_pairs={{8,0},{16,8},{24,16},{32,24},{40,32},{48,40},{56,48},{64,56},{72,6... | collective-permute-start | bytes 196616 | tf_op jit(solution)/shard_map/ppermute | solution.py:19
  7.3 1.9 collective-permute-done
  10.2 3.1 %collective-permute-start.3 = (bf16[4,6,1,128]{3,2,1,0:T(2,128)(2,1)S(1)}, bf16[4,6,1,128]{3,2,1,0:T(2,128)(2,1)S(1)}, u32[]{:S(2)}, u32[]{:S(2)}) collective-permute-start(bf16[4,6,1,128]{3,2,1,0:T(2,128)(2,1)S(1)} %get-tuple-element.34), channel_id=1, source_target_pairs={{2,0},{4,2},{6,4},{0,6},{3,1},{5,3},{7,5},{1,7},{10,8},{12,10},{14... | collective-permute-start | bytes 18440 | tf_op jit(solution)/shard_map/ppermute | solution.py:19
  13.3 1.4 collective-permute-done.3
  14.7 3.5 %collective-permute-done.2 = bf16[4,6,1,128]{3,2,1,0:T(2,128)(2,1)S(1)} collective-permute-done((bf16[4,6,1,128]{3,2,1,0:T(2,128)(2,1)S(1)}, bf16[4,6,1,128]{3,2,1,0:T(2,128)(2,1)S(1)}, u32[]{:S(2)}, u32[]{:S(2)}) %collective-permute-start.2) | collective-permute-done | bytes 6176 | tf_op jit(solution)/shard_map/ppermute | solution.py:17
  18.6 1.8 collective-permute-start.5
  20.9 1.7 copy.72
  22.7 7.9 %broadcast_in_dim.2 = f32[32,2,2,32,2,64,2]{0,6,5,4,3,2,1:T(2,128)} broadcast(f32[32,2,32,64]{0,3,2,1:T(8,128)S(1)} %copy.72), dimensions={0,1,3,5} | broadcast | bytes 4718592 | tf_op jit(solution)/shard_map/broadcast_in_dim | solution.py:65
  30.5 11.4 %copy.73 = f32[32,4,64,128]{3,0,2,1:T(8,128)} copy(f32[32,4,64,128]{0,3,2,1:T(8,128)} %bitcast.435) | data formatting | bytes 8388608 | tf_op jit(solution)/shard_map/reshape | solution.py:69
  42.0 2.2 pad_maximum_fusion.3
  48.1 9.9 %convert_reduce_fusion = (f32[32]{0:T(128)S(1)}, bf16[32,4,64,128]{3,0,2,1:T(8,128)(2,1)S(1)}, f32[32,4,64,128]{3,0,2,1:T(8,128)}) fusion(f32[32,4,64,128]{3,0,2,1:T(8,128)S(1)} %copy-done.1, f32[32]{0:T(128)S(1)} %copy-done.13, bf16[32,108]{0,1:T(8,128)(2,1)S(1)} %reshape.26, bf16[108,4,64,128]{3,2,1,0:T(8,128)(2,1)S(1)} %bitcast.437), kind=kOutput, calls=%fused_computation.23 | convolution fusion | flops 248512480 | bytes 17570816 | tf_op jit(solution)/shard_map/ok,kxyz->oxyz/dot_general | solution.py:56
  57.9 6.6 %fusion.167 = f32[32,108]{0,1:T(8,128)S(1)} fusion(bf16[32,4,64,128]{3,0,2,1:T(8,128)(2,1)S(1)} %get-tuple-element.19, bf16[108,4,64,128]{3,2,1,0:T(8,128)(2,1)S(1)} %bitcast.438), kind=kOutput, calls=%fused_computation.110 | convolution fusion | flops 226492416 | bytes 9188864 | tf_op jit(solution)/shard_map/oxyz,kxyz->ok/dot_general | solution.py:71
  65.6 10.5 %copy.71 = f32[32,4,64,128]{0,3,2,1:T(8,128)} copy(f32[32,4,64,128]{3,0,2,1:T(8,128)} %get-tuple-element.20) | data formatting | bytes 8388608 | tf_op jit(solution)/shard_map/add | solution.py:27
  76.1 3.1 %collective-permute-start.7 = (bf16[32,1,64,128]{3,0,2,1:T(8,128)(2,1)}, bf16[32,1,64,128]{3,0,2,1:T(8,128)(2,1)S(1)}, u32[]{:S(2)}, u32[]{:S(2)}) collective-permute-start(bf16[32,1,64,128]{3,0,2,1:T(8,128)(2,1)} %get-tuple-element.28), channel_id=1, source_target_pairs={{8,0},{16,8},{24,16},{32,24},{40,32},{48,40},{56,48},{64,56},{72,6... | collective-permute-start | bytes 1572872 | tf_op jit(solution)/shard_map/ppermute | solution.py:19
  79.2 13.1 %reduce_sum.18 = f32[32,2,32,64]{0,3,2,1:T(8,128)} reduce(f32[32,2,2,32,2,64,2]{0,6,5,4,3,2,1:T(2,128)} %bitcast.436, f32[]{:T(128)} %constant.2.clone.1), dimensions={2,4,6}, to_apply=%region_0.1 | reduce | flops 917504 | bytes 4718596 | tf_op jit(solution)/shard_map/reduce_sum | solution.py:62
  92.3 2.9 %multiply_convert_fusion = bf16[32,2,32,64]{0,3,2,1:T(8,128)(2,1)} fusion(f32[32,2,32,64]{0,3,2,1:T(8,128)} %reduce_sum.18), kind=kLoop, calls=%fused_computation.72 | loop fusion | flops 262144 | bytes 786432 | tf_op jit(solution)/shard_map/convert_element_type | solution.py:63
  95.1 2.8 %copy.80 = bf16[32,2,32,64]{3,2,1,0:T(8,128)(2,1)} copy(bf16[32,2,32,64]{0,3,2,1:T(8,128)(2,1)} %multiply_convert_fusion) | data formatting | bytes 524288
  97.9 68.2 %all-reduce = (f32[32,4,3,3,3]{0,4,3,2,1:T(4,128)S(1)}, f32[32]{0:T(128)}) all-reduce(f32[32,4,3,3,3]{0,4,3,2,1:T(4,128)S(1)} %reshape.29, f32[32]{0:T(128)S(1)} %get-tuple-element.18), channel_id=1, replica_groups=mesh['gx'=16,'gy'=4,'gz'=2] {'gx','gy','gz'}, use_global_device_ids=true, to_apply=%region_1.2 | all-reduce | flops 3488 | bytes 27904 | tf_op jit(solution)/shard_map/psum | solution.py:73
  168.9 1.3 collective-permute-start.8
  170.2 1.2 fusion.95
  171.4 1.2 fusion.18
  172.6 1.6 collective-permute-done.8
  174.9 4.1 %fusion.271 = (bf16[32,6,66,1]{3,0,2,1:T(8,128)(2,1)}, bf16[32,6,66,1]{3,0,2,1:T(8,128)(2,1)}) fusion(bf16[32,6,66,128]{3,0,2,1:T(8,128)(2,1)S(1)} %pad_maximum_fusion.1), kind=kLoop, calls=%fused_computation.251 | loop fusion | bytes 101376 | tf_op jit(solution)/shard_map/slice | solution.py:14
  179.0 4.8 %copy.76 = bf16[32,6,66,1]{2,0,3,1:T(8,128)(2,1)S(1)} copy(bf16[32,6,66,1]{3,0,2,1:T(8,128)(2,1)} %get-tuple-element.23) | data formatting | bytes 50688 | tf_op jit(solution)/shard_map/slice | solution.py:14
  185.0 4.8 %copy.78 = bf16[32,6,66,1]{2,0,3,1:T(8,128)(2,1)S(1)} copy(bf16[32,6,66,1]{3,0,2,1:T(8,128)(2,1)} %get-tuple-element.24) | data formatting | bytes 50688 | tf_op jit(solution)/shard_map/slice | solution.py:13
  191.9 1.2 convolution_bitcast_fusion.1
  193.1 1.2 fusion.219
  196.7 1.2 fusion.238
  197.9 6.0 %copy.77 = bf16[32,6,66,1]{3,0,2,1:T(8,128)(2,1)} copy(bf16[32,6,66,1]{2,0,3,1:T(8,128)(2,1)S(1)} %collective-permute-done.10) | data formatting | bytes 50688 | tf_op jit(solution)/shard_map/ppermute | solution.py:17
  203.9 6.0 %copy.79 = bf16[32,6,66,1]{3,0,2,1:T(8,128)(2,1)} copy(bf16[32,6,66,1]{2,0,3,1:T(8,128)(2,1)S(1)} %collective-permute-done.11) | data formatting | bytes 50688 | tf_op jit(solution)/shard_map/ppermute | solution.py:19
  209.9 9.5 %maximum_maximum_fusion = (bf16[32,6,66,129]{3,0,2,1:T(8,128)(2,1)S(1)}, bf16[32,6,66,129]{3,0,2,1:T(8,128)(2,1)S(1)}) fusion(bf16[32,6,1,128]{3,0,2,1:T(8,128)(2,1)S(1)} %collective-permute-done.9, bf16[32,1,64,128]{3,0,2,1:T(8,128)(2,1)S(1)} %collective-permute-done.7, bf16[32,4,64,128]{3,0,2,1:T(8,128)(2,1)S(1)} %get-tuple-element.19, ...), kind=kLoop, calls=%fused_computation.5 | loop fusion | flops 39232512 | bytes 9833472 | tf_op jit(solution)/shard_map/concatenate | solution.py:15
  230.4 1.4 fusion.146
  (106 shorter events, 28.4 us)
Async XLA Ops:
  1.5 7.6 %collective-permute-start = (bf16[4,1,64,128]{3,2,1,0:T(8,128)(2,1)S(1)}, bf16[4,1,64,128]{3,2,1,0:T(8,128)(2,1)S(1)}, u32[]{:S(2)}, u32[]{:S(2)}) collective-permute-start(bf16[4,1,64,128]{3,2,1,0:T(8,128)(2,1)S(1)} %get-tuple-element.36), channel_id=1, source_target_pairs={{0,8},{8,16},{16,24},{24,32},{32,40},{40,48},{48,56},{56,64},{64,7... | collective-permute-start | bytes 196616 | tf_op jit(solution)/shard_map/ppermute | solution.py:17
  1.6 8.5 %collective-permute-start.1 = (bf16[4,1,64,128]{3,2,1,0:T(8,128)(2,1)S(1)}, bf16[4,1,64,128]{3,2,1,0:T(8,128)(2,1)S(1)}, u32[]{:S(2)}, u32[]{:S(2)}) collective-permute-start(bf16[4,1,64,128]{3,2,1,0:T(8,128)(2,1)S(1)} %get-tuple-element.35), channel_id=1, source_target_pairs={{8,0},{16,8},{24,16},{32,24},{40,32},{48,40},{56,48},{64,56},{72,6... | collective-permute-start | bytes 196616 | tf_op jit(solution)/shard_map/ppermute | solution.py:19
  10.2 4.5 %collective-permute-start.3 = (bf16[4,6,1,128]{3,2,1,0:T(2,128)(2,1)S(1)}, bf16[4,6,1,128]{3,2,1,0:T(2,128)(2,1)S(1)}, u32[]{:S(2)}, u32[]{:S(2)}) collective-permute-start(bf16[4,6,1,128]{3,2,1,0:T(2,128)(2,1)S(1)} %get-tuple-element.34), channel_id=1, source_target_pairs={{2,0},{4,2},{6,4},{0,6},{3,1},{5,3},{7,5},{1,7},{10,8},{12,10},{14... | collective-permute-start | bytes 18440 | tf_op jit(solution)/shard_map/ppermute | solution.py:19
  13.3 4.9 %collective-permute-start.2 = (bf16[4,6,1,128]{3,2,1,0:T(2,128)(2,1)S(1)}, bf16[4,6,1,128]{3,2,1,0:T(2,128)(2,1)S(1)}, u32[]{:S(2)}, u32[]{:S(2)}) collective-permute-start(bf16[4,6,1,128]{3,2,1,0:T(2,128)(2,1)S(1)} %get-tuple-element.33), channel_id=1, source_target_pairs={{0,2},{2,4},{4,6},{6,0},{1,3},{3,5},{5,7},{7,1},{8,10},{10,12},{12... | collective-permute-start | bytes 18440 | tf_op jit(solution)/shard_map/ppermute | solution.py:17
  18.6 23.5 %collective-permute-start.5 = (bf16[4,6,66,1]{3,2,1,0:T(8,128)(2,1)S(1)}, bf16[4,6,66,1]{3,2,1,0:T(8,128)(2,1)}, u32[]{:S(2)}, u32[]{:S(2)}) collective-permute-start(bf16[4,6,66,1]{3,2,1,0:T(8,128)(2,1)S(1)} %get-tuple-element.29), channel_id=1, source_target_pairs={{1,0},{0,1},{3,2},{2,3},{5,4},{4,5},{7,6},{6,7},{9,8},{8,9},{11,10... | collective-permute-start | bytes 9512 | tf_op jit(solution)/shard_map/ppermute | solution.py:19
  20.4 21.6 %collective-permute-start.4 = (bf16[4,6,66,1]{3,2,1,0:T(8,128)(2,1)S(1)}, bf16[4,6,66,1]{3,2,1,0:T(8,128)(2,1)}, u32[]{:S(2)}, u32[]{:S(2)}) collective-permute-start(bf16[4,6,66,1]{3,2,1,0:T(8,128)(2,1)S(1)} %get-tuple-element.30), channel_id=1, source_target_pairs={{0,1},{1,0},{2,3},{3,2},{4,5},{5,4},{6,7},{7,6},{8,9},{9,8},{10,11... | collective-permute-start | bytes 9512 | tf_op jit(solution)/shard_map/ppermute | solution.py:17
  30.5 11.4 %copy-start.11 = (bf16[32,4,3,3,3]{0,1,4,3,2:T(4,128)(2,1)S(1)}, bf16[32,4,3,3,3]{0,1,4,3,2:T(4,128)(2,1)}, u32[]{:S(2)}) copy-start(bf16[32,4,3,3,3]{0,1,4,3,2:T(4,128)(2,1)} %param.5) | copy-start | bytes 20740
  30.5 14.2 %copy-start = (bf16[4,4,64,128]{3,2,1,0:T(8,128)(2,1)S(1)}, bf16[4,4,64,128]{3,2,1,0:T(8,128)(2,1)}, u32[]{:S(2)}) copy-start(bf16[4,4,64,128]{3,2,1,0:T(8,128)(2,1)} %param.4) | copy-start | bytes 786436
  44.8 3.3 %copy-start.1 = (f32[32,4,64,128]{3,0,2,1:T(8,128)S(1)}, f32[32,4,64,128]{3,0,2,1:T(8,128)}, u32[]{:S(2)}) copy-start(f32[32,4,64,128]{3,0,2,1:T(8,128)} %copy.73) | copy-start | bytes 12582916
  44.8 3.3 %copy-start.13 = (f32[32]{0:T(128)S(1)}, f32[32]{0:T(128)}, u32[]{:S(2)}) copy-start(f32[32]{0:T(128)} %param.6) | copy-start | bytes 388
  76.1 91.8 %collective-permute-start.7 = (bf16[32,1,64,128]{3,0,2,1:T(8,128)(2,1)}, bf16[32,1,64,128]{3,0,2,1:T(8,128)(2,1)S(1)}, u32[]{:S(2)}, u32[]{:S(2)}) collective-permute-start(bf16[32,1,64,128]{3,0,2,1:T(8,128)(2,1)} %get-tuple-element.28), channel_id=1, source_target_pairs={{8,0},{16,8},{24,16},{32,24},{40,32},{48,40},{56,48},{64,56},{72,6... | collective-permute-start | bytes 1572872 | tf_op jit(solution)/shard_map/ppermute | solution.py:19
  79.2 88.7 %collective-permute-start.6 = (bf16[32,1,64,128]{3,0,2,1:T(8,128)(2,1)}, bf16[32,1,64,128]{3,0,2,1:T(8,128)(2,1)S(1)}, u32[]{:S(2)}, u32[]{:S(2)}) collective-permute-start(bf16[32,1,64,128]{3,0,2,1:T(8,128)(2,1)} %get-tuple-element.27), channel_id=1, source_target_pairs={{0,8},{8,16},{16,24},{24,32},{32,40},{40,48},{48,56},{56,64},{64,7... | collective-permute-start | bytes 1572872 | tf_op jit(solution)/shard_map/ppermute | solution.py:17
  79.2 87.6 %copy-start.12 = (bf16[32,4,3,3,3]{0,1,4,3,2:T(4,128)(2,1)S(1)}, bf16[32,4,3,3,3]{0,1,4,3,2:T(4,128)(2,1)}, u32[]{:S(2)}) copy-start(bf16[32,4,3,3,3]{0,1,4,3,2:T(4,128)(2,1)} %param.5) | copy-start | bytes 20740
  167.9 4.7 %collective-permute-start.9 = (bf16[32,6,1,128]{3,0,2,1:T(8,128)(2,1)S(1)}, bf16[32,6,1,128]{3,0,2,1:T(8,128)(2,1)S(1)}, u32[]{:S(2)}, u32[]{:S(2)}) collective-permute-start(bf16[32,6,1,128]{3,0,2,1:T(8,128)(2,1)S(1)} %get-tuple-element.26), channel_id=1, source_target_pairs={{2,0},{4,2},{6,4},{0,6},{3,1},{5,3},{7,5},{1,7},{10,8},{12,10},{14... | collective-permute-start | bytes 147464 | tf_op jit(solution)/shard_map/ppermute | solution.py:19
  168.9 5.3 %collective-permute-start.8 = (bf16[32,6,1,128]{3,0,2,1:T(8,128)(2,1)S(1)}, bf16[32,6,1,128]{3,0,2,1:T(8,128)(2,1)S(1)}, u32[]{:S(2)}, u32[]{:S(2)}) collective-permute-start(bf16[32,6,1,128]{3,0,2,1:T(8,128)(2,1)S(1)} %get-tuple-element.25), channel_id=1, source_target_pairs={{0,2},{2,4},{4,6},{6,0},{1,3},{3,5},{5,7},{7,1},{8,10},{10,12},{12... | collective-permute-start | bytes 147464 | tf_op jit(solution)/shard_map/ppermute | solution.py:17
  183.8 14.1 %collective-permute-start.10 = (bf16[32,6,66,1]{2,0,3,1:T(8,128)(2,1)S(1)}, bf16[32,6,66,1]{2,0,3,1:T(8,128)(2,1)S(1)}, u32[]{:S(2)}, u32[]{:S(2)}) collective-permute-start(bf16[32,6,66,1]{2,0,3,1:T(8,128)(2,1)S(1)} %copy.76), channel_id=1, source_target_pairs={{0,1},{1,0},{2,3},{3,2},{4,5},{5,4},{6,7},{7,6},{8,9},{9,8},{10,11... | collective-permute-start | bytes 76040 | tf_op jit(solution)/shard_map/ppermute | solution.py:17
  189.7 14.2 %collective-permute-start.11 = (bf16[32,6,66,1]{2,0,3,1:T(8,128)(2,1)S(1)}, bf16[32,6,66,1]{2,0,3,1:T(8,128)(2,1)S(1)}, u32[]{:S(2)}, u32[]{:S(2)}) collective-permute-start(bf16[32,6,66,1]{2,0,3,1:T(8,128)(2,1)S(1)} %copy.78), channel_id=1, source_target_pairs={{1,0},{0,1},{3,2},{2,3},{5,4},{4,5},{7,6},{6,7},{9,8},{8,9},{11,10... | collective-permute-start | bytes 76040 | tf_op jit(solution)/shard_map/ppermute | solution.py:19
  226.0 3.4 %copy-start.2 = (f32[4,64,128,4]{2,3,1,0:T(4,128)S(1)}, f32[4,64,128,4]{2,3,1,0:T(4,128)}, u32[]{:S(2)}) copy-start(f32[4,64,128,4]{2,3,1,0:T(4,128)} %fusion.223) | copy-start | bytes 1572868
  226.0 3.4 %copy-start.4 = (f32[4,64,128,4]{2,3,1,0:T(4,128)S(1)}, f32[4,64,128,4]{2,3,1,0:T(4,128)}, u32[]{:S(2)}) copy-start(f32[4,64,128,4]{2,3,1,0:T(4,128)} %fusion.18) | copy-start | bytes 1572868
  226.0 3.4 %copy-start.8 = (f32[4,64,128,4]{2,3,1,0:T(4,128)S(1)}, f32[4,64,128,4]{2,3,1,0:T(4,128)}, u32[]{:S(2)}) copy-start(f32[4,64,128,4]{2,3,1,0:T(4,128)} %fusion.227) | copy-start | bytes 1572868
  226.0 3.4 %copy-start.9 = (f32[4,64,128,4]{2,3,1,0:T(4,128)S(1)}, f32[4,64,128,4]{2,3,1,0:T(4,128)}, u32[]{:S(2)}) copy-start(f32[4,64,128,4]{2,3,1,0:T(4,128)} %fusion.231) | copy-start | bytes 1572868
  226.0 3.4 %copy-start.10 = (f32[4,64,128,4]{2,3,1,0:T(4,128)S(1)}, f32[4,64,128,4]{2,3,1,0:T(4,128)}, u32[]{:S(2)}) copy-start(f32[4,64,128,4]{2,3,1,0:T(4,128)} %fusion.238) | copy-start | bytes 1572868
  228.5 1.9 copy-start.3
  228.5 1.9 copy-start.5
  228.5 1.9 copy-start.6
  228.5 1.9 copy-start.7
where the time goes:
time: 236 us; the launch traced here: 233 us
  blocking collectives  68.2 us (29%)
  local copies, waits for them, and re-layouts  67.6 us (29%)
  matrix products  39.4 us (17%)
  other arithmetic  29.3 us (12%)
  starting transfers between devices  18.7 us (8%)
  waiting for transfers between devices  8.38 us (4%)
    psum x1, blocking collectives, on_device(): lax.psum((weight_local, bias_local), ('gx', 'gy', 'gz'))  68.2 us
    dot_general x27, matrix products, on_device(): jnp.einsum('oc,oxyz->cxyz', weight[:, :, 2 - sa, 2 - sb, 2 - se], window,...  22.9 us
    ppermute x6, starting transfers between devices, extended(): lax.ppermute(head, axis, [((i + 1) % count, i) for i in range(count)])  15.6 us
    reduce_sum x1, other arithmetic, on_device(): pooled = activated.reshape(chan_out, cells_x // 2, 2, cells_y // 2, 2, ce...  13.1 us
    concatenate x4, other arithmetic, extended(): jnp.concatenate([lax.ppermute(tail, axis, [(i, (i + 1) % count) for i in...  12.6 us
    reshape x1, local copies, waits for them, and re-layouts, on_device(): spread = spread.reshape(chan_out, cells_x, cells_y, cells_z)  11.4 us
    add x1, local copies, waits for them, and re-layouts, activate(): leak_slope * preact  10.5 us
    slice x4, local copies, waits for them, and re-layouts, extended(): lax.slice_in_dim(cells, cells.shape[dim] - width, cells.shape[dim], axis=...  9.99 us
  transfers between devices with their start and end apart: 12, of which 4 were waited for; matrix products, arithmetic and copies ran while one was open for 27% of the time, Pallas kernels for 0%

commit v1 on v0

--- a/solution.py
+++ b/solution.py
@@ -70,7 +70,7 @@
     delta = (slope_of(preact) * spread * 0.125).astype(jnp.bfloat16)
     weight_local = jnp.einsum("oxyz,kxyz->ok", delta, patches, preferred_element_type=jnp.float32)
     bias_local = jnp.sum(delta, axis=(1, 2, 3), dtype=jnp.float32)
-    weight_total, bias_grad = lax.psum((weight_local, bias_local), ("gx", "gy", "gz"))
+    weight_total, bias_grad = lax.psum(lax.psum((weight_local, bias_local), "gx"), ("gy", "gz"))
     weight_grad = weight_total.reshape(chan_out, chan_in, 3, 3, 3)
     delta_wide = extended(delta, (("gx", 1), ("gy", 2), ("gz", 3)), 1)
     input_grad = jnp.zeros((chan_in, cells_x, cells_y, cells_z), jnp.float32)

time: 236 us -> 271 us (1.15)
  blocking collectives: 68.2 us -> 103 us
    psum x1 -> x2, blocking collectives: 68.2 us -> 103 us  [the longest x1 70.1 us: on_device(): lax.psum((weight_local, bias_local), 'gx')]
  transfers between devices with their start and end apart: 12 -> 12, of which waited for: 4 -> 4; matrix products, arithmetic and copies ran while one was open for 27% -> 24% of each run, Pallas kernels for 0% -> 0%
where the time goes in v1:
time: 271 us; the launch traced here: 267 us
  blocking collectives  103 us (38%)
  local copies, waits for them, and re-layouts  67.6 us (25%)
  matrix products  39.5 us (15%)
  other arithmetic  29.3 us (11%)
  starting transfers between devices  18.7 us (7%)
  waiting for transfers between devices  8.14 us (3%)
    psum x1, blocking collectives, on_device(): lax.psum((weight_local, bias_local), 'gx')  70.1 us
    psum x1, blocking collectives, on_device(): lax.psum(lax.psum((weight_local, bias_local), 'gx'), ('gy', 'gz'))  32.4 us
    dot_general x27, matrix products, on_device(): jnp.einsum('oc,oxyz->cxyz', weight[:, :, 2 - sa, 2 - sb, 2 - se], window,...  22.9 us
    ppermute x6, starting transfers between devices, extended(): lax.ppermute(head, axis, [((i + 1) % count, i) for i in range(count)])  15.1 us
    reduce_sum x1, other arithmetic, on_device(): pooled = activated.reshape(chan_out, cells_x // 2, 2, cells_y // 2, 2, ce...  13.1 us
    concatenate x4, other arithmetic, extended(): jnp.concatenate([lax.ppermute(tail, axis, [(i, (i + 1) % count) for i in...  12.6 us
    reshape x1, local copies, waits for them, and re-layouts, on_device(): spread = spread.reshape(chan_out, cells_x, cells_y, cells_z)  11.4 us
    add x1, local copies, waits for them, and re-layouts, activate(): leak_slope * preact  10.5 us
  transfers between devices with their start and end apart: 12, of which 4 were waited for; matrix products, arithmetic and copies ran while one was open for 24% of the time, Pallas kernels for 0%

profile of v1, /device:TPU:0, one launch (start us, length us, event | category | flops | bytes accessed | tf_op | source)
XLA Modules:
  0.0 267.2 jit_solution(14323319255518121149)
XLA Ops:
  1.6 5.7 %collective-permute-start.1 = (bf16[4,1,64,128]{3,2,1,0:T(8,128)(2,1)S(1)}, bf16[4,1,64,128]{3,2,1,0:T(8,128)(2,1)S(1)}, u32[]{:S(2)}, u32[]{:S(2)}) collective-permute-start(bf16[4,1,64,128]{3,2,1,0:T(8,128)(2,1)S(1)} %get-tuple-element.37), channel_id=1, source_target_pairs={{8,0},{16,8},{24,16},{32,24},{40,32},{48,40},{56,48},{64,56},{72,6... | collective-permute-start | bytes 196616 | tf_op jit(solution)/shard_map/ppermute | solution.py:19
  7.3 1.9 collective-permute-done
  10.2 3.1 %collective-permute-start.3 = (bf16[4,6,1,128]{3,2,1,0:T(2,128)(2,1)S(1)}, bf16[4,6,1,128]{3,2,1,0:T(2,128)(2,1)S(1)}, u32[]{:S(2)}, u32[]{:S(2)}) collective-permute-start(bf16[4,6,1,128]{3,2,1,0:T(2,128)(2,1)S(1)} %get-tuple-element.36), channel_id=1, source_target_pairs={{2,0},{4,2},{6,4},{0,6},{3,1},{5,3},{7,5},{1,7},{10,8},{12,10},{14... | collective-permute-start | bytes 18440 | tf_op jit(solution)/shard_map/ppermute | solution.py:19
  13.3 1.4 collective-permute-done.3
  14.7 3.5 %collective-permute-done.2 = bf16[4,6,1,128]{3,2,1,0:T(2,128)(2,1)S(1)} collective-permute-done((bf16[4,6,1,128]{3,2,1,0:T(2,128)(2,1)S(1)}, bf16[4,6,1,128]{3,2,1,0:T(2,128)(2,1)S(1)}, u32[]{:S(2)}, u32[]{:S(2)}) %collective-permute-start.2) | collective-permute-done | bytes 6176 | tf_op jit(solution)/shard_map/ppermute | solution.py:17
  18.6 1.8 collective-permute-start.5
  20.9 1.7 copy.72
  22.7 7.9 %broadcast_in_dim.2 = f32[32,2,2,32,2,64,2]{0,6,5,4,3,2,1:T(2,128)} broadcast(f32[32,2,32,64]{0,3,2,1:T(8,128)S(1)} %copy.72), dimensions={0,1,3,5} | broadcast | bytes 4718592 | tf_op jit(solution)/shard_map/broadcast_in_dim | solution.py:65
  30.5 11.4 %copy.73 = f32[32,4,64,128]{3,0,2,1:T(8,128)} copy(f32[32,4,64,128]{0,3,2,1:T(8,128)} %bitcast.437) | data formatting | bytes 8388608 | tf_op jit(solution)/shard_map/reshape | solution.py:69
  42.0 2.2 pad_maximum_fusion.3
  48.0 9.9 %convert_reduce_fusion = (f32[32]{0:T(128)S(1)}, bf16[32,4,64,128]{3,0,2,1:T(8,128)(2,1)S(1)}, f32[32,4,64,128]{3,0,2,1:T(8,128)}) fusion(f32[32,4,64,128]{3,0,2,1:T(8,128)S(1)} %copy-done.1, f32[32]{0:T(128)S(1)} %copy-done.13, bf16[32,108]{0,1:T(8,128)(2,1)S(1)} %reshape.26, bf16[108,4,64,128]{3,2,1,0:T(8,128)(2,1)S(1)} %bitcast.439), kind=kOutput, calls=%fused_computation.23 | convolution fusion | flops 248512480 | bytes 17570816 | tf_op jit(solution)/shard_map/ok,kxyz->oxyz/dot_general | solution.py:56
  57.9 6.8 %fusion.167 = f32[32,108]{1,0:T(8,128)S(1)} fusion(bf16[32,4,64,128]{3,0,2,1:T(8,128)(2,1)S(1)} %get-tuple-element.21, bf16[108,4,64,128]{3,2,1,0:T(8,128)(2,1)S(1)} %bitcast.440), kind=kOutput, calls=%fused_computation.110 | convolution fusion | flops 226492416 | bytes 9188864 | tf_op jit(solution)/shard_map/oxyz,kxyz->ok/dot_general | solution.py:71
  65.7 10.5 %copy.71 = f32[32,4,64,128]{0,3,2,1:T(8,128)} copy(f32[32,4,64,128]{3,0,2,1:T(8,128)} %get-tuple-element.22) | data formatting | bytes 8388608 | tf_op jit(solution)/shard_map/add | solution.py:27
  76.2 3.1 %collective-permute-start.7 = (bf16[32,1,64,128]{3,0,2,1:T(8,128)(2,1)}, bf16[32,1,64,128]{3,0,2,1:T(8,128)(2,1)S(1)}, u32[]{:S(2)}, u32[]{:S(2)}) collective-permute-start(bf16[32,1,64,128]{3,0,2,1:T(8,128)(2,1)} %get-tuple-element.30), channel_id=1, source_target_pairs={{8,0},{16,8},{24,16},{32,24},{40,32},{48,40},{56,48},{64,56},{72,6... | collective-permute-start | bytes 1572872 | tf_op jit(solution)/shard_map/ppermute | solution.py:19
  79.3 13.1 %reduce_sum.18 = f32[32,2,32,64]{0,3,2,1:T(8,128)} reduce(f32[32,2,2,32,2,64,2]{0,6,5,4,3,2,1:T(2,128)} %bitcast.438, f32[]{:T(128)} %constant.2.clone.1), dimensions={2,4,6}, to_apply=%region_0.1 | reduce | flops 917504 | bytes 4718596 | tf_op jit(solution)/shard_map/reduce_sum | solution.py:62
  92.3 2.9 %multiply_convert_fusion = bf16[32,2,32,64]{0,3,2,1:T(8,128)(2,1)} fusion(f32[32,2,32,64]{0,3,2,1:T(8,128)} %reduce_sum.18), kind=kLoop, calls=%fused_computation.72 | loop fusion | flops 262144 | bytes 786432 | tf_op jit(solution)/shard_map/convert_element_type | solution.py:63
  95.2 2.8 %copy.80 = bf16[32,2,32,64]{3,2,1,0:T(8,128)(2,1)} copy(bf16[32,2,32,64]{0,3,2,1:T(8,128)(2,1)} %multiply_convert_fusion) | data formatting | bytes 524288
  98.0 70.1 %all-reduce = (f32[32,108]{1,0:T(8,128)S(1)}, f32[32]{0:T(128)S(1)}) all-reduce(f32[32,108]{1,0:T(8,128)S(1)} %fusion.167, f32[32]{0:T(128)S(1)} %get-tuple-element.20), channel_id=1, replica_groups=mesh['gx'=16,'gy'=4,'gz'=2] {'gx'}, use_global_device_ids=true, to_apply=%region_1.2 | all-reduce | flops 3488 | bytes 27904 | tf_op jit(solution)/shard_map/psum | solution.py:73
  168.3 32.4 %all-reduce.1 = (f32[32,4,3,3,3]{0,4,3,2,1:T(4,128)S(1)}, f32[32]{0:T(128)}) all-reduce(f32[32,4,3,3,3]{0,4,3,2,1:T(4,128)S(1)} %reshape.29, f32[32]{0:T(128)S(1)} %get-tuple-element.17), channel_id=1, replica_groups=mesh['gx'=16,'gy'=4,'gz'=2] {'gy','gz'}, use_global_device_ids=true, to_apply=%region_2.3 | all-reduce | flops 3488 | bytes 27904 | tf_op jit(solution)/shard_map/psum | solution.py:73
  203.1 1.7 collective-permute-start.8
  206.0 1.2 fusion.18
  207.2 1.4 collective-permute-done.8
  209.2 4.1 %fusion.271 = (bf16[32,6,66,1]{3,0,2,1:T(8,128)(2,1)}, bf16[32,6,66,1]{3,0,2,1:T(8,128)(2,1)}) fusion(bf16[32,6,66,128]{3,0,2,1:T(8,128)(2,1)S(1)} %pad_maximum_fusion.1), kind=kLoop, calls=%fused_computation.251 | loop fusion | bytes 101376 | tf_op jit(solution)/shard_map/slice | solution.py:14
  213.4 4.8 %copy.76 = bf16[32,6,66,1]{2,0,3,1:T(8,128)(2,1)S(1)} copy(bf16[32,6,66,1]{3,0,2,1:T(8,128)(2,1)} %get-tuple-element.25) | data formatting | bytes 50688 | tf_op jit(solution)/shard_map/slice | solution.py:14
  218.1 1.3 collective-permute-start.10
  219.5 4.8 %copy.78 = bf16[32,6,66,1]{2,0,3,1:T(8,128)(2,1)S(1)} copy(bf16[32,6,66,1]{3,0,2,1:T(8,128)(2,1)} %get-tuple-element.26) | data formatting | bytes 50688 | tf_op jit(solution)/shard_map/slice | solution.py:13
  226.2 1.2 convolution_bitcast_fusion.1
  227.5 1.2 fusion.219
  232.2 6.0 %copy.77 = bf16[32,6,66,1]{3,0,2,1:T(8,128)(2,1)} copy(bf16[32,6,66,1]{2,0,3,1:T(8,128)(2,1)S(1)} %collective-permute-done.10) | data formatting | bytes 50688 | tf_op jit(solution)/shard_map/ppermute | solution.py:17
  238.3 6.0 %copy.79 = bf16[32,6,66,1]{3,0,2,1:T(8,128)(2,1)} copy(bf16[32,6,66,1]{2,0,3,1:T(8,128)(2,1)S(1)} %collective-permute-done.11) | data formatting | bytes 50688 | tf_op jit(solution)/shard_map/ppermute | solution.py:19
  244.3 9.5 %maximum_maximum_fusion = (bf16[32,6,66,129]{3,0,2,1:T(8,128)(2,1)S(1)}, bf16[32,6,66,129]{3,0,2,1:T(8,128)(2,1)S(1)}) fusion(bf16[32,6,1,128]{3,0,2,1:T(8,128)(2,1)S(1)} %collective-permute-done.9, bf16[32,1,64,128]{3,0,2,1:T(8,128)(2,1)S(1)} %collective-permute-done.7, bf16[32,4,64,128]{3,0,2,1:T(8,128)(2,1)S(1)} %get-tuple-element.21, ...), kind=kLoop, calls=%fused_computation.5 | loop fusion | flops 39232512 | bytes 9833472 | tf_op jit(solution)/shard_map/concatenate | solution.py:15
  264.7 1.4 fusion.146
  (108 shorter events, 29.1 us)
Async XLA Ops:
  1.5 7.6 %collective-permute-start = (bf16[4,1,64,128]{3,2,1,0:T(8,128)(2,1)S(1)}, bf16[4,1,64,128]{3,2,1,0:T(8,128)(2,1)S(1)}, u32[]{:S(2)}, u32[]{:S(2)}) collective-permute-start(bf16[4,1,64,128]{3,2,1,0:T(8,128)(2,1)S(1)} %get-tuple-element.38), channel_id=1, source_target_pairs={{0,8},{8,16},{16,24},{24,32},{32,40},{40,48},{48,56},{56,64},{64,7... | collective-permute-start | bytes 196616 | tf_op jit(solution)/shard_map/ppermute | solution.py:17
  1.6 8.5 %collective-permute-start.1 = (bf16[4,1,64,128]{3,2,1,0:T(8,128)(2,1)S(1)}, bf16[4,1,64,128]{3,2,1,0:T(8,128)(2,1)S(1)}, u32[]{:S(2)}, u32[]{:S(2)}) collective-permute-start(bf16[4,1,64,128]{3,2,1,0:T(8,128)(2,1)S(1)} %get-tuple-element.37), channel_id=1, source_target_pairs={{8,0},{16,8},{24,16},{32,24},{40,32},{48,40},{56,48},{64,56},{72,6... | collective-permute-start | bytes 196616 | tf_op jit(solution)/shard_map/ppermute | solution.py:19
  10.2 4.5 %collective-permute-start.3 = (bf16[4,6,1,128]{3,2,1,0:T(2,128)(2,1)S(1)}, bf16[4,6,1,128]{3,2,1,0:T(2,128)(2,1)S(1)}, u32[]{:S(2)}, u32[]{:S(2)}) collective-permute-start(bf16[4,6,1,128]{3,2,1,0:T(2,128)(2,1)S(1)} %get-tuple-element.36), channel_id=1, source_target_pairs={{2,0},{4,2},{6,4},{0,6},{3,1},{5,3},{7,5},{1,7},{10,8},{12,10},{14... | collective-permute-start | bytes 18440 | tf_op jit(solution)/shard_map/ppermute | solution.py:19
  13.3 4.9 %collective-permute-start.2 = (bf16[4,6,1,128]{3,2,1,0:T(2,128)(2,1)S(1)}, bf16[4,6,1,128]{3,2,1,0:T(2,128)(2,1)S(1)}, u32[]{:S(2)}, u32[]{:S(2)}) collective-permute-start(bf16[4,6,1,128]{3,2,1,0:T(2,128)(2,1)S(1)} %get-tuple-element.35), channel_id=1, source_target_pairs={{0,2},{2,4},{4,6},{6,0},{1,3},{3,5},{5,7},{7,1},{8,10},{10,12},{12... | collective-permute-start | bytes 18440 | tf_op jit(solution)/shard_map/ppermute | solution.py:17
  18.6 23.4 %collective-permute-start.5 = (bf16[4,6,66,1]{3,2,1,0:T(8,128)(2,1)S(1)}, bf16[4,6,66,1]{3,2,1,0:T(8,128)(2,1)}, u32[]{:S(2)}, u32[]{:S(2)}) collective-permute-start(bf16[4,6,66,1]{3,2,1,0:T(8,128)(2,1)S(1)} %get-tuple-element.31), channel_id=1, source_target_pairs={{1,0},{0,1},{3,2},{2,3},{5,4},{4,5},{7,6},{6,7},{9,8},{8,9},{11,10... | collective-permute-start | bytes 9512 | tf_op jit(solution)/shard_map/ppermute | solution.py:19
  20.4 21.6 %collective-permute-start.4 = (bf16[4,6,66,1]{3,2,1,0:T(8,128)(2,1)S(1)}, bf16[4,6,66,1]{3,2,1,0:T(8,128)(2,1)}, u32[]{:S(2)}, u32[]{:S(2)}) collective-permute-start(bf16[4,6,66,1]{3,2,1,0:T(8,128)(2,1)S(1)} %get-tuple-element.32), channel_id=1, source_target_pairs={{0,1},{1,0},{2,3},{3,2},{4,5},{5,4},{6,7},{7,6},{8,9},{9,8},{10,11... | collective-permute-start | bytes 9512 | tf_op jit(solution)/shard_map/ppermute | solution.py:17
  30.5 11.4 %copy-start.11 = (bf16[32,4,3,3,3]{0,1,4,3,2:T(4,128)(2,1)S(1)}, bf16[32,4,3,3,3]{0,1,4,3,2:T(4,128)(2,1)}, u32[]{:S(2)}) copy-start(bf16[32,4,3,3,3]{0,1,4,3,2:T(4,128)(2,1)} %param.5) | copy-start | bytes 20740
  30.5 14.2 %copy-start = (bf16[4,4,64,128]{3,2,1,0:T(8,128)(2,1)S(1)}, bf16[4,4,64,128]{3,2,1,0:T(8,128)(2,1)}, u32[]{:S(2)}) copy-start(bf16[4,4,64,128]{3,2,1,0:T(8,128)(2,1)} %param.4) | copy-start | bytes 786436
  44.8 3.3 %copy-start.1 = (f32[32,4,64,128]{3,0,2,1:T(8,128)S(1)}, f32[32,4,64,128]{3,0,2,1:T(8,128)}, u32[]{:S(2)}) copy-start(f32[32,4,64,128]{3,0,2,1:T(8,128)} %copy.73) | copy-start | bytes 12582916
  44.8 3.3 %copy-start.13 = (f32[32]{0:T(128)S(1)}, f32[32]{0:T(128)}, u32[]{:S(2)}) copy-start(f32[32]{0:T(128)} %param.6) | copy-start | bytes 388
  76.2 126.3 %collective-permute-start.7 = (bf16[32,1,64,128]{3,0,2,1:T(8,128)(2,1)}, bf16[32,1,64,128]{3,0,2,1:T(8,128)(2,1)S(1)}, u32[]{:S(2)}, u32[]{:S(2)}) collective-permute-start(bf16[32,1,64,128]{3,0,2,1:T(8,128)(2,1)} %get-tuple-element.30), channel_id=1, source_target_pairs={{8,0},{16,8},{24,16},{32,24},{40,32},{48,40},{56,48},{64,56},{72,6... | collective-permute-start | bytes 1572872 | tf_op jit(solution)/shard_map/ppermute | solution.py:19
  79.3 123.2 %collective-permute-start.6 = (bf16[32,1,64,128]{3,0,2,1:T(8,128)(2,1)}, bf16[32,1,64,128]{3,0,2,1:T(8,128)(2,1)S(1)}, u32[]{:S(2)}, u32[]{:S(2)}) collective-permute-start(bf16[32,1,64,128]{3,0,2,1:T(8,128)(2,1)} %get-tuple-element.29), channel_id=1, source_target_pairs={{0,8},{8,16},{16,24},{24,32},{32,40},{40,48},{48,56},{56,64},{64,7... | collective-permute-start | bytes 1572872 | tf_op jit(solution)/shard_map/ppermute | solution.py:17
  79.3 122.1 %copy-start.12 = (bf16[32,4,3,3,3]{0,1,4,3,2:T(4,128)(2,1)S(1)}, bf16[32,4,3,3,3]{0,1,4,3,2:T(4,128)(2,1)}, u32[]{:S(2)}) copy-start(bf16[32,4,3,3,3]{0,1,4,3,2:T(4,128)(2,1)} %param.5) | copy-start | bytes 20740
  202.5 4.7 %collective-permute-start.9 = (bf16[32,6,1,128]{3,0,2,1:T(8,128)(2,1)S(1)}, bf16[32,6,1,128]{3,0,2,1:T(8,128)(2,1)S(1)}, u32[]{:S(2)}, u32[]{:S(2)}) collective-permute-start(bf16[32,6,1,128]{3,0,2,1:T(8,128)(2,1)S(1)} %get-tuple-element.28), channel_id=1, source_target_pairs={{2,0},{4,2},{6,4},{0,6},{3,1},{5,3},{7,5},{1,7},{10,8},{12,10},{14... | collective-permute-start | bytes 147464 | tf_op jit(solution)/shard_map/ppermute | solution.py:19
  203.1 5.5 %collective-permute-start.8 = (bf16[32,6,1,128]{3,0,2,1:T(8,128)(2,1)S(1)}, bf16[32,6,1,128]{3,0,2,1:T(8,128)(2,1)S(1)}, u32[]{:S(2)}, u32[]{:S(2)}) collective-permute-start(bf16[32,6,1,128]{3,0,2,1:T(8,128)(2,1)S(1)} %get-tuple-element.27), channel_id=1, source_target_pairs={{0,2},{2,4},{4,6},{6,0},{1,3},{3,5},{5,7},{7,1},{8,10},{10,12},{12... | collective-permute-start | bytes 147464 | tf_op jit(solution)/shard_map/ppermute | solution.py:17
  218.1 14.1 %collective-permute-start.10 = (bf16[32,6,66,1]{2,0,3,1:T(8,128)(2,1)S(1)}, bf16[32,6,66,1]{2,0,3,1:T(8,128)(2,1)S(1)}, u32[]{:S(2)}, u32[]{:S(2)}) collective-permute-start(bf16[32,6,66,1]{2,0,3,1:T(8,128)(2,1)S(1)} %copy.76), channel_id=1, source_target_pairs={{0,1},{1,0},{2,3},{3,2},{4,5},{5,4},{6,7},{7,6},{8,9},{9,8},{10,11... | collective-permute-start | bytes 76040 | tf_op jit(solution)/shard_map/ppermute | solution.py:17
  224.2 14.0 %collective-permute-start.11 = (bf16[32,6,66,1]{2,0,3,1:T(8,128)(2,1)S(1)}, bf16[32,6,66,1]{2,0,3,1:T(8,128)(2,1)S(1)}, u32[]{:S(2)}, u32[]{:S(2)}) collective-permute-start(bf16[32,6,66,1]{2,0,3,1:T(8,128)(2,1)S(1)} %copy.78), channel_id=1, source_target_pairs={{1,0},{0,1},{3,2},{2,3},{5,4},{4,5},{7,6},{6,7},{9,8},{8,9},{11,10... | collective-permute-start | bytes 76040 | tf_op jit(solution)/shard_map/ppermute | solution.py:19
  260.3 3.4 %copy-start.2 = (f32[4,64,128,4]{2,3,1,0:T(4,128)S(1)}, f32[4,64,128,4]{2,3,1,0:T(4,128)}, u32[]{:S(2)}) copy-start(f32[4,64,128,4]{2,3,1,0:T(4,128)} %fusion.223) | copy-start | bytes 1572868
  260.3 3.4 %copy-start.4 = (f32[4,64,128,4]{2,3,1,0:T(4,128)S(1)}, f32[4,64,128,4]{2,3,1,0:T(4,128)}, u32[]{:S(2)}) copy-start(f32[4,64,128,4]{2,3,1,0:T(4,128)} %fusion.18) | copy-start | bytes 1572868
  260.4 3.4 %copy-start.8 = (f32[4,64,128,4]{2,3,1,0:T(4,128)S(1)}, f32[4,64,128,4]{2,3,1,0:T(4,128)}, u32[]{:S(2)}) copy-start(f32[4,64,128,4]{2,3,1,0:T(4,128)} %fusion.227) | copy-start | bytes 1572868
  260.4 3.4 %copy-start.9 = (f32[4,64,128,4]{2,3,1,0:T(4,128)S(1)}, f32[4,64,128,4]{2,3,1,0:T(4,128)}, u32[]{:S(2)}) copy-start(f32[4,64,128,4]{2,3,1,0:T(4,128)} %fusion.231) | copy-start | bytes 1572868
  260.4 3.4 %copy-start.10 = (f32[4,64,128,4]{2,3,1,0:T(4,128)S(1)}, f32[4,64,128,4]{2,3,1,0:T(4,128)}, u32[]{:S(2)}) copy-start(f32[4,64,128,4]{2,3,1,0:T(4,128)} %fusion.238) | copy-start | bytes 1572868
  262.8 1.9 copy-start.3
  262.8 1.9 copy-start.5
  262.9 1.9 copy-start.6
  262.9 1.9 copy-start.7
